TPU v7x, 128 devices: a whole 4x4x4 slice. The times are simulated.
128 devices in a mesh: own: 8 (over y_lo, x), dp: 16 (over y_hi, z, core).
Axes of the slice: x: 4, y: 4 (y_hi: 2, y_lo: 2; y = y_hi * 2 + y_lo), z: 4, core: 2. Of those that a mesh axis runs over, the one named last changes fastest.
Arguments:
- tokens: bfloat16 [16384, 1536], P('dp'), may hold values from -6 to 6
- assign: int32 [128, 2], P('dp'), may hold values from 0 to 7, all different within a row; in each aligned block of 8 rows (0 to 7, 8 to 15, ...) at most 5 rows name the same one
- gates: float32 [16384, 2], P('dp'), may hold values from 0.25 to 1
- cot: bfloat16 [16384, 1536], P('dp', 'own'), may hold values from -1.75 to 1.75
- w_in: bfloat16 [8, 1536, 2048], P('own', None, 'dp'), may hold values from -0.15625 to 0.15625
- w_out: bfloat16 [8, 2048, 1536], P('own', 'dp'), may hold values from -0.125 to 0.125
Outputs:
- mixed: bfloat16 [16384, 1536], P('dp', 'own')
- grad_tokens: bfloat16 [16384, 1536], P('dp', 'own')
- grad_w_in: float32 [8, 1536, 2048], P('own', None, 'dp')
- grad_w_out: float32 [8, 2048, 1536], P('own', 'dp')
Inputs may be any that keep to these rules, and one draw needn't show every extreme that they name: `assign`: the two entries of a block name different experts. Among the 8 blocks of one index of dp no expert is named more than 5 times, and in every draw some expert is named exactly 5 times by the blocks of some index of dp.
All inputs are finite; a program needn't handle non-finite values.
Results may differ from a plain program's by a relative error of at most 0.012.
Values may be sent and summed in bfloat16 or wider, within the bound.
No kernel may reach another device: no remote copies, remote signals or barrier semaphores. Data moves between devices by JAX's collectives and lax.ppermute only.
A program may use at most 128 MiB of HBM per device.

v0:
```python
import jax
import jax.numpy as jnp
from jax import lax
from jax.sharding import PartitionSpec as P

CAP = 5


def pick_blocks(assign_rows, expert, capacity):
    hit_flag = jnp.logical_or(assign_rows[:, 0] == expert, assign_rows[:, 1] == expert).astype(
        jnp.int32
    )
    slot_rank = jnp.cumsum(hit_flag) - 1
    slot_ids = jnp.arange(capacity, dtype=jnp.int32)
    matches = jnp.logical_and(
        hit_flag[None, :] == 1, slot_rank[None, :] == slot_ids[:, None]
    ).astype(jnp.int32)
    where_idx = jnp.arange(assign_rows.shape[0], dtype=jnp.int32)
    blocks = jnp.sum(matches * where_idx[None, :], axis=1)
    is_valid = jnp.sum(matches, axis=1).astype(jnp.float32)
    return (blocks, is_valid)


def block_gates(assign_rows, gate_blocks, blocks, is_valid, expert):
    chosen = assign_rows[blocks]
    picked_gates = gate_blocks[blocks]
    first_hit = (chosen[:, 0] == expert).astype(jnp.float32)
    second_hit = (chosen[:, 1] == expert).astype(jnp.float32)
    mixing = picked_gates[..., 0] * first_hit[:, None] + picked_gates[..., 1] * second_hit[:, None]
    return mixing * is_valid[:, None]


def gelu_cdf(values):
    return 0.5 * (1.0 + jax.scipy.special.erf(values * 0.7071067811865476))


def gelu_slope(values):
    return gelu_cdf(values) + values * jnp.exp(-0.5 * values * values) * 0.3989422804014327


def place_rows(terms, blocks, block_count):
    block_len = terms.shape[-2]
    width = terms.shape[-1]
    zeros = jnp.zeros((block_count, block_len, width), jnp.float32)
    placed = zeros.at[blocks.reshape(-1)].add(terms.reshape(-1, block_len, width))
    return placed.reshape(block_count * block_len, width)


def body(tokens, assign, gates, cot, w_in, w_out):
    own_count = w_in.shape[0]
    block_count = assign.shape[0]
    block_len = tokens.shape[0] // block_count
    width = tokens.shape[1]
    full_in, full_out = (
        lax.all_gather(w_in, "dp", axis=2, tiled=True),
        lax.all_gather(w_out, "dp", axis=1, tiled=True),
    )
    expert_ids = lax.axis_index("own") * own_count + jnp.arange(own_count, dtype=jnp.int32)
    blocks, is_valid = jax.vmap(pick_blocks, (None, 0, None))(assign, expert_ids, CAP)
    gate_blocks = gates.reshape(block_count, block_len, 2)
    mixing = jax.vmap(block_gates, (None, None, 0, 0, 0))(
        assign, gate_blocks, blocks, is_valid, expert_ids
    )
    weight_rows = mixing.reshape(own_count, CAP * block_len)
    token_blocks = tokens.reshape(block_count, block_len, width)
    picked = token_blocks[blocks].reshape(own_count, CAP * block_len, width)
    pre_act = jnp.einsum("erd,edf->erf", picked, full_in, preferred_element_type=jnp.float32)
    hidden = (pre_act * gelu_cdf(pre_act)).astype(jnp.bfloat16)
    expert_out = jnp.einsum("erf,efd->erd", hidden, full_out, preferred_element_type=jnp.float32)
    contrib = (weight_rows[..., None] * expert_out).reshape(own_count, CAP, block_len, width)
    partial_rows = place_rows(contrib, blocks, block_count)
    mixed = lax.psum_scatter(
        partial_rows.astype(jnp.bfloat16), "own", scatter_dimension=1, tiled=True
    )
    cot_full = lax.all_gather(cot, "own", axis=1, tiled=True)
    cot_picked = cot_full.reshape(block_count, block_len, width)[blocks].reshape(
        own_count, CAP * block_len, width
    )
    grad_out = (weight_rows[..., None] * cot_picked.astype(jnp.float32)).astype(jnp.bfloat16)
    grad_hidden = jnp.einsum("erd,efd->erf", grad_out, full_out, preferred_element_type=jnp.float32)
    grad_pre = (grad_hidden * gelu_slope(pre_act)).astype(jnp.bfloat16)
    grad_in_terms = jnp.einsum(
        "erf,edf->erd", grad_pre, full_in, preferred_element_type=jnp.float32
    )
    grad_rows = place_rows(
        grad_in_terms.reshape(own_count, CAP, block_len, width), blocks, block_count
    )
    grad_tokens = lax.psum_scatter(
        grad_rows.astype(jnp.bfloat16), "own", scatter_dimension=1, tiled=True
    )
    out_full = jnp.einsum("erf,erd->efd", hidden, grad_out, preferred_element_type=jnp.float32)
    in_full = jnp.einsum("erf,erd->efd", grad_pre, picked, preferred_element_type=jnp.float32)
    grad_w_out, in_shard = (
        lax.psum_scatter(
            out_full.astype(jnp.bfloat16), "dp", scatter_dimension=1, tiled=True
        ).astype(jnp.float32),
        lax.psum_scatter(
            in_full.astype(jnp.bfloat16), "dp", scatter_dimension=1, tiled=True
        ).astype(jnp.float32),
    )
    grad_w_in = jnp.transpose(in_shard, (0, 2, 1))
    return (mixed, grad_tokens, grad_w_in, grad_w_out)


def solution(mesh):
    placed = (
        P("dp", None),
        P("dp", None),
        P("dp", None),
        P("dp", "own"),
        P("own", None, "dp"),
        P("own", "dp", None),
    )
    return jax.shard_map(
        body,
        mesh=mesh,
        in_specs=placed,
        out_specs=(P("dp", "own"), P("dp", "own"), P("own", None, "dp"), P("own", "dp", None)),
        check_vma=False,
    )
```

profile of v0, /device:TPU:0, one launch (start us, length us, event | category | flops | bytes accessed | tf_op | source)
XLA Modules:
  0.0 489.7 jit_solution(8797572180045873756)
XLA Ops:
  10.2 0.8 compare_bitcast_fusion
  12.1 1.3 gather_fusion
  13.4 2.2 gather_fusion.2
  15.8 40.3 %all-gather.8.cloned.1.call-done = bf16[1024,1536]{0,1:T(8,128)(2,1)} async-done(((bf16[1024,192]{0,1:T(8,128)(2,1)}), bf16[1024,1536]{0,1:T(8,128)(2,1)}) %all-gather.8.cloned.1.call-update) | async-done | bytes 3145744 | tf_op jit(solution)/shard_map/all_gather | solution.py:75
  56.1 3.2 copy.22
  59.3 2.1 gather_fusion.3
  61.4 63.2 %all-gather.4.cloned.1.call-done = bf16[1,1536,2048]{2,1,0:T(8,128)(2,1)} async-done(((bf16[1,1536,128]{2,1,0:T(8,128)(2,1)}), bf16[1,1536,2048]{2,1,0:T(8,128)(2,1)}) %all-gather.4.cloned.1.call-update) | async-done | bytes 6291472 | tf_op jit(solution)/shard_map/all_gather | solution.py:55
  124.6 9.2 %multiply_convert_fusion = (bf16[640,2048]{1,0:T(8,128)(2,1)}, f32[640,2048]{1,0:T(8,128)}) fusion(bf16[640,1536]{1,0:T(8,128)(2,1)} %bitcast.89, bf16[1,1536,2048]{2,1,0:T(8,128)(2,1)} %all-gather.4.cloned.1.call-done), kind=kOutput, calls=%fused_computation.25 | convolution fusion | flops 4033085440 | bytes 16121856 | tf_op jit(solution)/shard_map/erd,edf->erf/dot_general | solution.py:67
  133.8 54.6 %all-gather.6.cloned.1.call-done = bf16[1,2048,1536]{2,1,0:T(8,128)(2,1)} async-done(((bf16[1,128,1536]{2,1,0:T(8,128)(2,1)}), bf16[1,2048,1536]{2,1,0:T(8,128)(2,1)}) %all-gather.6.cloned.1.call-update) | async-done | bytes 6291472 | tf_op jit(solution)/shard_map/all_gather | solution.py:56
  188.5 8.4 %fusion.15 = bf16[640,2048]{1,0:T(8,128)(2,1)S(1)} fusion(f32[640,2048]{1,0:T(8,128)} %get-tuple-element.25, bf16[1,2048,1536]{2,1,0:T(8,128)(2,1)} %all-gather.6.cloned.1.call-done, f32[640]{0:T(1024)S(1)} %bitcast_multiply_fusion.1, bf16[1,640,1,1,1,1,1536]{6,1,5,4,3,2,0:T(8,128)(2,1)S(1)} %bitcast.87), kind=kOutput, calls=%fused_computation.24 | convolution fusion | flops 4042588160 | bytes 16124416 | tf_op jit(solution)/shard_map/erd,efd->erf/dot_general | solution.py:80
  196.9 1.6 copy-done.4
  198.4 7.0 %fusion = bf16[1,2048,1536]{2,1,0:T(8,128)(2,1)} fusion(bf16[640,2048]{1,0:T(8,128)(2,1)S(1)} %fusion.15, bf16[640,1536]{1,0:T(8,128)(2,1)S(1)} %bitcast.90), kind=kOutput, calls=%fused_computation.9 | convolution fusion | flops 4029677568 | bytes 10878976 | tf_op jit(solution)/shard_map/erf,erd->efd/dot_general | solution.py:92
  205.9 1.3 copy-done.6
  207.3 7.0 %fusion.1 = bf16[1,2048,1536]{2,1,0:T(8,128)(2,1)} fusion(bf16[640,2048]{1,0:T(8,128)(2,1)S(1)} %copy-done.6, bf16[640,1536]{1,0:T(8,128)(2,1)S(1)} %fusion.16), kind=kOutput, calls=%fused_computation.10 | convolution fusion | flops 4029677568 | bytes 10878976 | tf_op jit(solution)/shard_map/erf,erd->efd/dot_general | solution.py:91
  214.5 1.7 copy-done.5
  216.2 9.4 %fusion.2 = f32[5,128,1536]{2,1,0:T(8,128)} fusion(bf16[5,128,2048]{2,1,0:T(8,128)(2,1)S(1)} %bitcast.92, bf16[1,1536,2048]{2,1,0:T(8,128)(2,1)} %all-gather.4.cloned.1.call-done), kind=kOutput, calls=%fused_computation.11 | convolution fusion | flops 4026531840 | bytes 12845056 | tf_op jit(solution)/shard_map/erf,edf->erd/dot_general | solution.py:82
  225.6 3.4 broadcast.269.clone.1
  229.0 10.4 %scatter_fusion.1 = f32[8,128,1536]{2,1,0:T(8,128)} fusion(f32[8,128,1536]{2,1,0:T(8,128)} %broadcast.269.clone.1, s32[5]{0:T(128)S(1)} %fusion.28, f32[5,128,1536]{2,1,0:T(8,128)} %fusion.2), kind=kCustom, calls=%fused_computation.5 | custom fusion | flops 983040 | bytes 11796500 | tf_op jit(solution)/shard_map/scatter-add | solution.py:45
  239.3 3.2 convert_element_type.158
  242.5 3.0 copy.23
  245.6 9.8 %fusion.17 = f32[640,1536]{1,0:T(8,128)} fusion(bf16[640,2048]{1,0:T(8,128)(2,1)} %get-tuple-element.24, bf16[1,2048,1536]{2,1,0:T(8,128)(2,1)} %all-gather.6.cloned.1.call-done, f32[640]{0:T(1024)S(1)} %bitcast_multiply_fusion.1), kind=kOutput, calls=%fused_computation.30 | convolution fusion | flops 4027514880 | bytes 12847616 | tf_op jit(solution)/shard_map/erf,efd->erd/dot_general | solution.py:69
  255.4 3.5 broadcast.269.clone
  258.8 10.4 %scatter_fusion = f32[8,128,1536]{2,1,0:T(8,128)} fusion(f32[8,128,1536]{2,1,0:T(8,128)} %broadcast.269.clone, s32[5]{0:T(128)S(1)} %fusion.28, f32[5,128,1536]{2,1,0:T(8,128)} %bitcast.88), kind=kCustom, calls=%fused_computation.4 | custom fusion | flops 983040 | bytes 11796500 | tf_op jit(solution)/shard_map/scatter-add | solution.py:45
  269.3 4.8 convert_element_type.151
  274.1 4.8 copy.21
  278.9 14.3 %reduce-scatter.9.cloned.1.call-done = bf16[1,128,1536]{2,1,0:T(8,128)(2,1)} async-done(((bf16[1,2048,1536]{2,1,0:T(8,128)(2,1)}), bf16[1,128,1536]{2,1,0:T(8,128)(2,1)}) %reduce-scatter.9.cloned.1.call-update) | async-done | bytes 393232 | tf_op jit(solution)/shard_map/reduce_scatter | solution.py:97
  293.2 2.0 convert_bitcast_fusion
  295.2 2.3 copy.24
  297.5 88.5 %reduce-scatter.11.cloned.1.call-done = bf16[1,128,1536]{2,1,0:T(8,128)(2,1)} async-done(((bf16[1,2048,1536]{2,1,0:T(8,128)(2,1)}), bf16[1,128,1536]{2,1,0:T(8,128)(2,1)}) %reduce-scatter.11.cloned.1.call-update) | async-done | bytes 393232 | tf_op jit(solution)/shard_map/reduce_scatter | solution.py:94
  386.0 2.0 convert_element_type.167
  387.9 46.1 %reduce-scatter.7.cloned.1.call-done = bf16[1024,192]{0,1:T(8,128)(2,1)} async-done(((bf16[1024,1536]{0,1:T(8,128)(2,1)}), bf16[1024,192]{0,1:T(8,128)(2,1)}) %reduce-scatter.7.cloned.1.call-update) | async-done | bytes 393232 | tf_op jit(solution)/shard_map/reduce_scatter | solution.py:88
  434.0 48.8 %reduce-scatter.5.cloned.1.call-done = bf16[1024,192]{0,1:T(8,128)(2,1)} async-done(((bf16[1024,1536]{0,1:T(8,128)(2,1)}), bf16[1024,192]{0,1:T(8,128)(2,1)}) %reduce-scatter.5.cloned.1.call-update) | async-done | bytes 393232 | tf_op jit(solution)/shard_map/reduce_scatter | solution.py:72
  (41 shorter events, 5.1 us)
Async XLA Ops:
  7.2 6.2 %copy-start = (bf16[1024,1536]{1,0:T(8,128)(2,1)S(1)}, bf16[1024,1536]{1,0:T(8,128)(2,1)}, u32[]{:S(2)}) copy-start(bf16[1024,1536]{1,0:T(8,128)(2,1)} %param.6) | copy-start | bytes 9437188
  7.2 48.9 %all-gather.8.cloned.1.call-start = ((), (), s32[]{:S(2)}) async-start(), calls=%async_computation.7 | async-start | bytes 3538944 | tf_op jit(solution)/shard_map/all_gather | solution.py:75
  7.9 116.7 %all-gather.4.cloned.1.call-start = ((), (), s32[]{:S(2)}) async-start(), calls=%async_computation.4 | async-start | bytes 6684672 | tf_op jit(solution)/shard_map/all_gather | solution.py:55
  8.7 179.8 %all-gather.6.cloned.1.call-start = ((), (), s32[]{:S(2)}) async-start(), calls=%async_computation.5 | async-start | bytes 6684672 | tf_op jit(solution)/shard_map/all_gather | solution.py:56
  9.4 283.8 %reduce-scatter.9.cloned.1.call-start = ((), (), s32[]{:S(2)}) async-start(), calls=%async_computation.9 | async-start | bytes 6684672 | tf_op jit(solution)/shard_map/reduce_scatter | solution.py:97
  124.6 63.8 %copy-start.2 = (bf16[5,128,1536]{2,1,0:T(8,128)(2,1)S(1)}, bf16[5,128,1536]{2,1,0:T(8,128)(2,1)}, u32[]{:S(2)}) copy-start(bf16[5,128,1536]{2,1,0:T(8,128)(2,1)} %gather_fusion.3) | copy-start | bytes 5898244
  188.5 10.0 %copy-start.3 = (bf16[5,128,1536]{2,1,0:T(8,128)(2,1)S(1)}, bf16[5,128,1536]{2,1,0:T(8,128)(2,1)}, u32[]{:S(2)}) copy-start(bf16[5,128,1536]{2,1,0:T(8,128)(2,1)} %gather_fusion.2) | copy-start | bytes 5898244
  196.9 1.6 copy-start.4
  205.5 180.5 %reduce-scatter.11.cloned.1.call-start = ((), (), s32[]{:S(2)}) async-start(), calls=%async_computation.10 | async-start | bytes 6684672 | tf_op jit(solution)/shard_map/reduce_scatter | solution.py:94
  205.5 1.7 copy-start.6
  214.2 1.9 copy-start.5
  214.3 219.7 %reduce-scatter.7.cloned.1.call-start = ((), (), s32[]{:S(2)}) async-start(), calls=%async_computation.8 | async-start | bytes 3538944 | tf_op jit(solution)/shard_map/reduce_scatter | solution.py:88
  245.5 237.3 %reduce-scatter.5.cloned.1.call-start = ((), (), s32[]{:S(2)}) async-start(), calls=%async_computation.6 | async-start | bytes 3538944 | tf_op jit(solution)/shard_map/reduce_scatter | solution.py:72
  274.1 208.8 %copy-start.1 = (bf16[1024,1536]{1,0:T(8,128)(2,1)S(1)}, bf16[1024,1536]{1,0:T(8,128)(2,1)}, u32[]{:S(2)}) copy-start(bf16[1024,1536]{1,0:T(8,128)(2,1)} %param.6) | copy-start | bytes 9437188
Sparse Core Ops, SparseCore 0:
  9.6 46.3 all-gather.7
  58.3 66.2 all-gather.3
  127.1 61.2 all-gather.5
  205.6 87.5 reduce-scatter.8
  297.3 88.6 reduce-scatter.10
  388.8 45.1 reduce-scatter.6
  437.0 45.7 reduce-scatter.4
where the time goes:
time: 490 us
  waiting for transfers between devices  358 us (73%)
  matrix products  50.8 us (10%)
  other arithmetic  34.4 us (7%)
  local copies, waits for them, and re-layouts  31.9 us (7%)
  between operations  14.3 us (3%)
    reduce_scatter x1, waiting for transfers between devices, body(): lax.psum_scatter(out_full.astype(jnp.bfloat16), 'dp', scatter_dimension=1...  88.5 us
    all_gather x1, waiting for transfers between devices, body(): lax.all_gather(w_in, 'dp', axis=2, tiled=True)  63.2 us
    all_gather x1, waiting for transfers between devices, body(): lax.all_gather(w_out, 'dp', axis=1, tiled=True)  54.6 us
    reduce_scatter x1, waiting for transfers between devices, body(): lax.psum_scatter(partial_rows.astype(jnp.bfloat16), 'own', scatter_dimens...  48.8 us
    reduce_scatter x1, waiting for transfers between devices, body(): lax.psum_scatter(grad_rows.astype(jnp.bfloat16), 'own', scatter_dimension...  46.1 us
    all_gather x1, waiting for transfers between devices, body(): cot_full = lax.all_gather(cot, 'own', axis=1, tiled=True)  40.3 us
    scatter-add x2, other arithmetic, place_rows(): zeros.at[blocks.reshape(-1)].add(terms.reshape(-1, block_len, width))  20.8 us
    reduce_scatter x1, waiting for transfers between devices, body(): lax.psum_scatter(in_full.astype(jnp.bfloat16), 'dp', scatter_dimension=1,...  14.3 us
  transfers between devices with their start and end apart: 7, of which 7 were waited for; matrix products, arithmetic and copies ran while one was open for 20% of the time, Pallas kernels for 0%

commit v1 on v0

--- a/solution.py
+++ b/solution.py
@@ -72,7 +72,9 @@
     mixed = lax.psum_scatter(
         partial_rows.astype(jnp.bfloat16), "own", scatter_dimension=1, tiled=True
     )
-    cot_full = lax.all_gather(cot, "own", axis=1, tiled=True)
+    cot_full = jnp.concatenate(
+        lax.all_to_all(jnp.stack([cot] * lax.axis_size("own")), "own", 0, 0), axis=1
+    )
     cot_picked = cot_full.reshape(block_count, block_len, width)[blocks].reshape(
         own_count, CAP * block_len, width
     )

time: 490 us -> 473 us (0.965)
  waiting for transfers between devices: 358 us -> 330 us
  starting transfers between devices: 0.46 us -> 6.2 us
  local copies, waits for them, and re-layouts: 31.9 us -> 37 us
    all_gather x1 -> x0, waiting for transfers between devices: 40.3 us -> none  [body(): cot_full = lax.all_gather(cot, 'own', axis=1, tiled=True)]
    all_to_all x0 -> x1, waiting for transfers between devices: none -> 35.9 us  [body(): lax.all_to_all(jnp.stack([cot] * lax.axis_size('own')), 'own', 0, 0)]
    all_gather x1, waiting for transfers between devices: 63.2 us -> 40.5 us  [body(): lax.all_gather(w_in, 'dp', axis=2, tiled=True)]
    another operation x2 -> x4, local copies, waits for them, and re-layouts: 6.83 us -> 13.3 us
    all_to_all x0 -> x1, starting transfers between devices: none -> 5.56 us  [body(): lax.all_to_all(jnp.stack([cot] * lax.axis_size('own')), 'own', 0, 0)]
    unnamed x16 -> x19, local copies, waits for them, and re-layouts: 7.64 us -> 9.86 us
  transfers between devices with their start and end apart: 7 -> 7, of which waited for: 7 -> 7; matrix products, arithmetic and copies ran while one was open for 20% -> 21% of each run, Pallas kernels for 0% -> 0%
where the time goes in v1:
time: 473 us; the launch traced here: 472 us
  waiting for transfers between devices  330 us (70%)
  matrix products  50.6 us (11%)
  local copies, waits for them, and re-layouts  37 us (8%)
  other arithmetic  33.7 us (7%)
  between operations  14.3 us (3%)
  starting transfers between devices  6.2 us (1%)
    reduce_scatter x1, waiting for transfers between devices, body(): lax.psum_scatter(out_full.astype(jnp.bfloat16), 'dp', scatter_dimension=1...  88.5 us
    all_gather x1, waiting for transfers between devices, body(): lax.all_gather(w_out, 'dp', axis=1, tiled=True)  54.8 us
    reduce_scatter x1, waiting for transfers between devices, body(): lax.psum_scatter(partial_rows.astype(jnp.bfloat16), 'own', scatter_dimens...  49.3 us
    reduce_scatter x1, waiting for transfers between devices, body(): lax.psum_scatter(grad_rows.astype(jnp.bfloat16), 'own', scatter_dimension...  46.1 us
    all_gather x1, waiting for transfers between devices, body(): lax.all_gather(w_in, 'dp', axis=2, tiled=True)  40.5 us
    all_to_all x1, waiting for transfers between devices, body(): lax.all_to_all(jnp.stack([cot] * lax.axis_size('own')), 'own', 0, 0)  35.9 us
    scatter-add x2, other arithmetic, place_rows(): zeros.at[blocks.reshape(-1)].add(terms.reshape(-1, block_len, width))  20.9 us
    reduce_scatter x1, waiting for transfers between devices, body(): lax.psum_scatter(in_full.astype(jnp.bfloat16), 'dp', scatter_dimension=1,...  13.8 us
  transfers between devices with their start and end apart: 7, of which 7 were waited for; matrix products, arithmetic and copies ran while one was open for 21% of the time, Pallas kernels for 0%

profile of v1, /device:TPU:0, one launch (start us, length us, event | category | flops | bytes accessed | tf_op | source)
XLA Modules:
  0.0 472.0 jit_solution(17091913122571755837)
XLA Ops:
  8.7 3.0 stack.2
  11.7 5.6 %all-to-all-start = ((bf16[8,1024,192]{1,2,0:T(8,128)(2,1)}), bf16[8,1024,192]{1,2,0:T(8,128)(2,1)}, u32[]{:S(2)}, u32[]{:S(2)}) async-start(bf16[8,1024,192]{1,2,0:T(8,128)(2,1)} %stack.2), calls=%async_computation.1 | async-start | bytes 6291456 | tf_op jit(solution)/shard_map/all_to_all | solution.py:76
  19.1 2.1 gather_fusion.2
  21.5 35.9 %all-to-all-done = bf16[8,1024,192]{1,2,0:T(8,128)(2,1)} async-done(((bf16[8,1024,192]{1,2,0:T(8,128)(2,1)}), bf16[8,1024,192]{1,2,0:T(8,128)(2,1)}, u32[]{:S(2)}, u32[]{:S(2)}) %all-to-all-start) | async-done | bytes 3145760 | tf_op jit(solution)/shard_map/all_to_all | solution.py:76
  57.4 2.7 copy.32
  60.1 3.4 copy.29
  63.5 2.6 gather_fusion.3
  66.1 40.5 %all-gather.3.cloned.1.call-done = bf16[1,1536,2048]{2,1,0:T(8,128)(2,1)} async-done(((bf16[1,1536,128]{2,1,0:T(8,128)(2,1)}), bf16[1,1536,2048]{2,1,0:T(8,128)(2,1)}) %all-gather.3.cloned.1.call-update) | async-done | bytes 6291472 | tf_op jit(solution)/shard_map/all_gather | solution.py:55
  106.5 9.1 %multiply_convert_fusion = (bf16[640,2048]{1,0:T(8,128)(2,1)}, f32[640,2048]{1,0:T(8,128)}) fusion(bf16[640,1536]{1,0:T(8,128)(2,1)} %bitcast.94, bf16[1,1536,2048]{2,1,0:T(8,128)(2,1)} %all-gather.3.cloned.1.call-done), kind=kOutput, calls=%fused_computation.25 | convolution fusion | flops 4033085440 | bytes 16121856 | tf_op jit(solution)/shard_map/erd,edf->erf/dot_general | solution.py:67
  115.6 54.8 %all-gather.5.cloned.1.call-done = bf16[1,2048,1536]{2,1,0:T(8,128)(2,1)} async-done(((bf16[1,128,1536]{2,1,0:T(8,128)(2,1)}), bf16[1,2048,1536]{2,1,0:T(8,128)(2,1)}) %all-gather.5.cloned.1.call-update) | async-done | bytes 6291472 | tf_op jit(solution)/shard_map/all_gather | solution.py:56
  170.4 8.4 %fusion.15 = bf16[640,2048]{1,0:T(8,128)(2,1)S(1)} fusion(f32[640,2048]{1,0:T(8,128)} %get-tuple-element.29, bf16[1,2048,1536]{2,1,0:T(8,128)(2,1)} %all-gather.5.cloned.1.call-done, f32[640]{0:T(1024)S(1)} %bitcast_multiply_fusion.1, bf16[1,640,1,1,1,1,1536]{6,1,5,4,3,2,0:T(8,128)(2,1)S(1)} %bitcast.92), kind=kOutput, calls=%fused_computation.24 | convolution fusion | flops 4042588160 | bytes 16124416 | tf_op jit(solution)/shard_map/erd,efd->erf/dot_general | solution.py:82
  178.8 1.6 copy-done.5
  180.3 7.0 %fusion = bf16[1,2048,1536]{2,1,0:T(8,128)(2,1)} fusion(bf16[640,2048]{1,0:T(8,128)(2,1)S(1)} %fusion.15, bf16[640,1536]{1,0:T(8,128)(2,1)S(1)} %bitcast.95), kind=kOutput, calls=%fused_computation.9 | convolution fusion | flops 4029677568 | bytes 10878976 | tf_op jit(solution)/shard_map/erf,erd->efd/dot_general | solution.py:94
  189.3 7.0 %fusion.1 = bf16[1,2048,1536]{2,1,0:T(8,128)(2,1)} fusion(bf16[640,2048]{1,0:T(8,128)(2,1)S(1)} %copy-done.7, bf16[640,1536]{1,0:T(8,128)(2,1)S(1)} %fusion.16), kind=kOutput, calls=%fused_computation.10 | convolution fusion | flops 4029677568 | bytes 10878976 | tf_op jit(solution)/shard_map/erf,erd->efd/dot_general | solution.py:93
  196.4 1.9 copy-done.6
  198.2 9.4 %fusion.2 = f32[5,128,1536]{2,1,0:T(8,128)} fusion(bf16[5,128,2048]{2,1,0:T(8,128)(2,1)S(1)} %bitcast.97, bf16[1,1536,2048]{2,1,0:T(8,128)(2,1)} %all-gather.3.cloned.1.call-done), kind=kOutput, calls=%fused_computation.11 | convolution fusion | flops 4026531840 | bytes 12845056 | tf_op jit(solution)/shard_map/erf,edf->erd/dot_general | solution.py:84
  207.7 3.4 broadcast.271.clone.1
  211.0 10.4 %scatter_fusion.1 = f32[8,128,1536]{2,1,0:T(8,128)} fusion(f32[8,128,1536]{2,1,0:T(8,128)} %broadcast.271.clone.1, s32[5]{0:T(128)S(1)} %fusion.28, f32[5,128,1536]{2,1,0:T(8,128)} %fusion.2), kind=kCustom, calls=%fused_computation.5 | custom fusion | flops 983040 | bytes 11796500 | tf_op jit(solution)/shard_map/scatter-add | solution.py:45
  221.4 3.2 convert_element_type.158
  224.6 3.0 copy.30
  227.9 9.8 %fusion.17 = f32[640,1536]{1,0:T(8,128)} fusion(bf16[640,2048]{1,0:T(8,128)(2,1)} %get-tuple-element.28, bf16[1,2048,1536]{2,1,0:T(8,128)(2,1)} %all-gather.5.cloned.1.call-done, f32[640]{0:T(1024)S(1)} %bitcast_multiply_fusion.1), kind=kOutput, calls=%fused_computation.30 | convolution fusion | flops 4027514880 | bytes 12847616 | tf_op jit(solution)/shard_map/erf,efd->erd/dot_general | solution.py:69
  237.7 3.5 broadcast.271.clone
  241.1 10.6 %scatter_fusion = f32[8,128,1536]{2,1,0:T(8,128)} fusion(f32[8,128,1536]{2,1,0:T(8,128)} %broadcast.271.clone, s32[5]{0:T(128)S(1)} %fusion.28, f32[5,128,1536]{2,1,0:T(8,128)} %bitcast.93), kind=kCustom, calls=%fused_computation.4 | custom fusion | flops 983040 | bytes 11796500 | tf_op jit(solution)/shard_map/scatter-add | solution.py:45
  251.7 4.8 %convert_element_type.151 = bf16[8,128,1536]{2,1,0:T(8,128)(2,1)} convert(f32[8,128,1536]{2,1,0:T(8,128)} %scatter_fusion) | non-fusion elementwise | flops 1572864 | bytes 9437184 | tf_op jit(solution)/shard_map/convert_element_type | solution.py:73
  256.4 4.9 %copy.28 = bf16[1024,1536]{0,1:T(8,128)(2,1)} copy(bf16[1024,1536]{1,0:T(8,128)(2,1)} %bitcast.91) | data formatting | bytes 6291456 | tf_op jit(solution)/shard_map/convert_element_type | solution.py:73
  261.3 13.8 %reduce-scatter.9.cloned.1.call-done = bf16[1,128,1536]{2,1,0:T(8,128)(2,1)} async-done(((bf16[1,2048,1536]{2,1,0:T(8,128)(2,1)}), bf16[1,128,1536]{2,1,0:T(8,128)(2,1)}) %reduce-scatter.9.cloned.1.call-update) | async-done | bytes 393232 | tf_op jit(solution)/shard_map/reduce_scatter | solution.py:99
  275.1 2.0 convert_bitcast_fusion
  277.1 2.3 copy.31
  279.3 88.5 %reduce-scatter.11.cloned.1.call-done = bf16[1,128,1536]{2,1,0:T(8,128)(2,1)} async-done(((bf16[1,2048,1536]{2,1,0:T(8,128)(2,1)}), bf16[1,128,1536]{2,1,0:T(8,128)(2,1)}) %reduce-scatter.11.cloned.1.call-update) | async-done | bytes 393232 | tf_op jit(solution)/shard_map/reduce_scatter | solution.py:96
  367.8 2.0 convert_element_type.167
  369.8 46.1 %reduce-scatter.7.cloned.1.call-done = bf16[1024,192]{0,1:T(8,128)(2,1)} async-done(((bf16[1024,1536]{0,1:T(8,128)(2,1)}), bf16[1024,192]{0,1:T(8,128)(2,1)}) %reduce-scatter.7.cloned.1.call-update) | async-done | bytes 393232 | tf_op jit(solution)/shard_map/reduce_scatter | solution.py:90
  415.9 49.3 %reduce-scatter.5.cloned.1.call-done = bf16[1024,192]{0,1:T(8,128)(2,1)} async-done(((bf16[1024,1536]{0,1:T(8,128)(2,1)}), bf16[1024,192]{0,1:T(8,128)(2,1)}) %reduce-scatter.5.cloned.1.call-update) | async-done | bytes 393232 | tf_op jit(solution)/shard_map/reduce_scatter | solution.py:72
  (44 shorter events, 5.8 us)
Async XLA Ops:
  7.2 12.0 %copy-start = (bf16[1024,1536]{1,0:T(8,128)(2,1)S(1)}, bf16[1024,1536]{1,0:T(8,128)(2,1)}, u32[]{:S(2)}) copy-start(bf16[1024,1536]{1,0:T(8,128)(2,1)} %param.6) | copy-start | bytes 9437188
  7.2 99.4 %all-gather.3.cloned.1.call-start = ((), (), s32[]{:S(2)}) async-start(), calls=%async_computation.5 | async-start | bytes 6684672 | tf_op jit(solution)/shard_map/all_gather | solution.py:55
  7.9 162.4 %all-gather.5.cloned.1.call-start = ((), (), s32[]{:S(2)}) async-start(), calls=%async_computation.6 | async-start | bytes 6684672 | tf_op jit(solution)/shard_map/all_gather | solution.py:56
  11.7 5.6 %copy-start.4 = (s32[8,2]{0,1:T(2,128)S(1)}, s32[8,2]{0,1:T(2,128)}, u32[]{:S(2)}) copy-start(s32[8,2]{0,1:T(2,128)} %param.7) | copy-start | bytes 196
  11.7 6.8 %copy-start.2 = (f32[1024,2]{0,1:T(2,128)S(1)}, f32[1024,2]{0,1:T(2,128)}, u32[]{:S(2)}) copy-start(f32[1024,2]{0,1:T(2,128)} %param.8) | copy-start | bytes 24580
  11.7 45.7 %all-to-all-start = ((bf16[8,1024,192]{1,2,0:T(8,128)(2,1)}), bf16[8,1024,192]{1,2,0:T(8,128)(2,1)}, u32[]{:S(2)}, u32[]{:S(2)}) async-start(bf16[8,1024,192]{1,2,0:T(8,128)(2,1)} %stack.2), calls=%async_computation.1 | async-start | bytes 6291456 | tf_op jit(solution)/shard_map/all_to_all | solution.py:76
  17.2 257.9 %reduce-scatter.9.cloned.1.call-start = ((), (), s32[]{:S(2)}) async-start(), calls=%async_computation.9 | async-start | bytes 6684672 | tf_op jit(solution)/shard_map/reduce_scatter | solution.py:99
  170.3 10.0 %copy-start.3 = (bf16[5,128,1536]{2,1,0:T(8,128)(2,1)S(1)}, bf16[5,128,1536]{2,1,0:T(8,128)(2,1)}, u32[]{:S(2)}) copy-start(bf16[5,128,1536]{2,1,0:T(8,128)(2,1)} %gather_fusion.2) | copy-start | bytes 5898244
  178.7 1.6 copy-start.5
  187.4 180.5 %reduce-scatter.11.cloned.1.call-start = ((), (), s32[]{:S(2)}) async-start(), calls=%async_computation.10 | async-start | bytes 6684672 | tf_op jit(solution)/shard_map/reduce_scatter | solution.py:96
  187.6 1.7 copy-start.7
  196.3 1.9 copy-start.6
  196.3 219.5 %reduce-scatter.7.cloned.1.call-start = ((), (), s32[]{:S(2)}) async-start(), calls=%async_computation.8 | async-start | bytes 3538944 | tf_op jit(solution)/shard_map/reduce_scatter | solution.py:90
  227.6 237.5 %reduce-scatter.5.cloned.1.call-start = ((), (), s32[]{:S(2)}) async-start(), calls=%async_computation.7 | async-start | bytes 3538944 | tf_op jit(solution)/shard_map/reduce_scatter | solution.py:72
  256.4 208.7 %copy-start.1 = (bf16[1024,1536]{1,0:T(8,128)(2,1)S(1)}, bf16[1024,1536]{1,0:T(8,128)(2,1)}, u32[]{:S(2)}) copy-start(bf16[1024,1536]{1,0:T(8,128)(2,1)} %param.6) | copy-start | bytes 9437188
Sparse Core Ops, SparseCore 0:
  10.3 96.2 all-gather.2
  109.0 61.2 all-gather.4
  187.5 87.5 reduce-scatter.8
  279.1 88.6 reduce-scatter.10
  370.7 45.1 reduce-scatter.6
  418.7 46.3 reduce-scatter.4
